TPU v7x, 128 devices: a whole 4x4x4 slice. The times are simulated.
128 devices in a mesh: tm: 32 (over y, x, core), blk: 4 (over z).
Axes of the slice: x: 4, y: 4, z: 4, core: 2. Of those that a mesh axis runs over, the one named last changes fastest.
Arguments:
- dynamics: float32 [256, 256], replicated
- dynamics_mask: int32 [8, 8], replicated, may hold values from 0 to 1, as said below
- obs_op: float32 [256, 256], replicated, may hold values from -0.375 to 0.375
- obs_mask: int32 [8, 8], replicated, may hold values from 0 to 1, as said below
- process_noise: float32 [256], replicated, may hold values from 0.0005 to 0.005
- initial_expectation: float32 [256], replicated, may hold values from -6 to 6
- filter_gains: float32 [512, 256, 256], P('tm', 'blk'), may hold values from -0.009765625 to 0.009765625
- observations: float32 [512, 256], P('tm'), may hold values from -6 to 6
- smooth_gains: float32 [512, 256, 256], P('tm', 'blk')
- filt_cov: float32 [512, 256, 256], P('tm', 'blk')
Outputs:
- smoothed_means: float32 [512, 256], P('tm', 'blk')
- smoothed_cov: float32 [512, 256, 256], P('tm', 'blk')
Inputs may be any that keep to these rules, and one draw needn't show every extreme that they name: `dynamics_mask`: diagonal blocks are 1. `obs_mask`: blocks with equal row and column index are 1.
All inputs are finite; a program needn't handle non-finite values.
Results may differ from a plain program's by a relative error of at most 0.0003.
Values sent between devices are 32-bit elements; how exact they have to be, the bound alone decides.
A program may use at most 256 MiB of HBM per device.

v0:
```python
import jax
import jax.numpy as jnp
from jax import lax
from jax.sharding import PartitionSpec as P

highest = lax.Precision.HIGHEST


def from_behind(block, axis, distance):
    devices = range(lax.axis_size(axis))
    route = [(i - distance, i) for i in devices if i - distance in devices]
    return lax.ppermute(block, axis, route)


def expand_mask(mask, row_total, col_total):
    row_block = row_total // mask.shape[0]
    col_block = col_total // mask.shape[1]
    return jnp.repeat(jnp.repeat(mask.astype(jnp.float32), row_block, axis=0), col_block, axis=1)


def matmul(left, right):
    return jnp.matmul(left, right, precision=highest)


def filter_join(earlier, latter):
    return (matmul(latter[0], earlier[0]), matmul(latter[0], earlier[1]) + latter[1])


def smooth_join(earlier, latter):
    gain_late = latter[0]
    return (
        matmul(gain_late, earlier[0]),
        matmul(matmul(gain_late, earlier[1]), gain_late.T) + latter[1],
        matmul(gain_late, earlier[2]) + latter[2],
    )


def pack_filter(parts):
    return jnp.concatenate([parts[0], parts[1][None, :]], axis=0)


def unpack_filter(packed, width):
    return (packed[:width], packed[width])


def pack_smooth(parts):
    return jnp.concatenate([parts[0], parts[1], parts[2][None, :]], axis=0)


def unpack_smooth(packed, width):
    return (packed[:width], packed[width : 2 * width], packed[2 * width])


def window_work(
    trans_map,
    process_noise,
    initial_expectation,
    transition_operators,
    step_shifts,
    gain_full,
    cov_full,
    is_final,
    filter_prefix,
    smooth_prefix,
):
    width = trans_map.shape[0]
    step_count = transition_operators.shape[0]
    final_step = jnp.logical_and(is_final, jnp.arange(step_count) == step_count - 1)
    gain_full = jnp.where(final_step[:, None, None], jnp.float32(0.0), gain_full)
    ident_map = jnp.eye(width, dtype=jnp.float32)
    zero_mat = jnp.zeros((width, width), jnp.float32)
    zero_vec = jnp.zeros((width,), jnp.float32)

    def window_filter(running, step_parts):
        return (filter_join(running, step_parts), None)

    filt_window = lax.scan(
        window_filter, (ident_map, zero_vec), (transition_operators, step_shifts)
    )[0]
    filt_before = filter_prefix(filt_window)
    mean_in = matmul(filt_before[0], initial_expectation) + filt_before[1]

    def filter_walk(current, step_parts):
        current = matmul(step_parts[0], current) + step_parts[1]
        return (current, current)

    filt_means = lax.scan(filter_walk, mean_in, (transition_operators, step_shifts))[1]
    predicted = matmul(matmul(trans_map, cov_full), trans_map.T) + jnp.diag(process_noise)
    gain_trans = jnp.swapaxes(gain_full, 1, 2)
    residual_cov = cov_full - matmul(matmul(gain_full, predicted), gain_trans)
    moved_means = jnp.einsum("ij,tj->ti", trans_map, filt_means, precision=highest)
    offsets = filt_means - jnp.einsum("tij,tj->ti", gain_full, moved_means, precision=highest)

    def window_smooth(running, step_parts):
        return (smooth_join(running, step_parts), None)

    smooth_window = lax.scan(
        window_smooth,
        (ident_map, zero_mat, zero_vec),
        (gain_full, residual_cov, offsets),
        reverse=True,
    )[0]
    smooth_after = smooth_prefix(smooth_window)

    def smooth_walk(current, step_parts):
        cov_next, mean_next = current
        gain_now, resid_now, offset_now = step_parts
        cov_now = matmul(matmul(gain_now, cov_next), gain_now.T) + resid_now
        current_mean = matmul(gain_now, mean_next) + offset_now
        return ((cov_now, current_mean), (current_mean, cov_now))

    return lax.scan(
        smooth_walk,
        (smooth_after[1], smooth_after[2]),
        (gain_full, residual_cov, offsets),
        reverse=True,
    )[1]


def per_device(
    dynamics,
    dynamics_mask,
    obs_op,
    obs_mask,
    process_noise,
    initial_expectation,
    filter_gains,
    observations,
    smooth_gains,
    filt_cov,
):
    width = dynamics.shape[0]
    obs_width = obs_op.shape[0]
    row_count = filter_gains.shape[1]
    row_start = lax.axis_index("blk") * row_count
    trans_map = dynamics * expand_mask(dynamics_mask, width, width)
    obs_map = obs_op * expand_mask(obs_mask, obs_width, width)
    obs_dyn = matmul(obs_map, trans_map)
    own_rows = lax.dynamic_slice_in_dim(trans_map, row_start, row_count, 0)
    map_rows = own_rows[None] - matmul(filter_gains, obs_dyn)
    shift_rows = jnp.einsum("tro,to->tr", filter_gains, observations, precision=highest)
    ident_map = jnp.eye(width, dtype=jnp.float32)
    zero_mat = jnp.zeros((width, width), jnp.float32)
    zero_vec = jnp.zeros((width,), jnp.float32)
    transition_operators, step_shifts, gain_full, cov_full = (
        lax.all_gather(map_rows, "blk", axis=1, tiled=True),
        lax.all_gather(shift_rows, "blk", axis=1, tiled=True),
        lax.all_gather(smooth_gains, "blk", axis=1, tiled=True),
        lax.all_gather(filt_cov, "blk", axis=1, tiled=True),
    )
    tm_index = lax.axis_index("tm")
    tm_count = lax.axis_size("tm")

    def before_filter(filt_window):

        def chain_filter(turn_no, running):
            arrived = from_behind(pack_filter(filter_join(running, filt_window)), "tm", 1)
            parts = unpack_filter(arrived, width)
            first_window = tm_index == 0
            return (
                jnp.where(first_window, ident_map, parts[0]),
                jnp.where(first_window, zero_vec, parts[1]),
            )

        return lax.fori_loop(0, tm_count - 1, chain_filter, (ident_map, zero_vec))

    def after_smooth(smooth_window):

        def chain_smooth(turn_no, running):
            arrived = from_behind(pack_smooth(smooth_join(running, smooth_window)), "tm", -1)
            parts = unpack_smooth(arrived, width)
            last_window = tm_index == tm_count - 1
            return (
                jnp.where(last_window, ident_map, parts[0]),
                jnp.where(last_window, zero_mat, parts[1]),
                jnp.where(last_window, zero_vec, parts[2]),
            )

        return lax.fori_loop(0, tm_count - 1, chain_smooth, (ident_map, zero_mat, zero_vec))

    means_out, cov_out = window_work(
        trans_map,
        process_noise,
        initial_expectation,
        transition_operators,
        step_shifts,
        gain_full,
        cov_full,
        tm_index == tm_count - 1,
        before_filter,
        after_smooth,
    )
    means_rows = lax.dynamic_slice_in_dim(means_out, row_start, row_count, 1)
    cov_rows = lax.dynamic_slice_in_dim(cov_out, row_start, row_count, 1)
    return (means_rows, cov_rows)


def solution(mesh):
    return jax.shard_map(
        per_device,
        mesh=mesh,
        in_specs=(
            P(),
            P(),
            P(),
            P(),
            P(),
            P(),
            P("tm", "blk", None),
            P("tm", None),
            P("tm", "blk", None),
            P("tm", "blk", None),
        ),
        out_specs=(P("tm", "blk"), P("tm", "blk", None)),
        check_vma=False,
    )
```

profile of v0, /device:TPU:7, one launch (start us, length us, event | category | flops | bytes accessed | tf_op | source)
XLA Modules:
  0.0 1111.3 jit_solution(17786515966806534478)
XLA Ops:
  16.8 10.5 all-gather
  28.2 36.9 %all-gather.9.cloned.1.call-done = f32[16,256,256]{2,1,0:T(8,128)} async-done(((f32[16,64,256]{2,1,0:T(8,128)}), f32[16,256,256]{2,1,0:T(8,128)}) %all-gather.9.cloned.1.call-update) | async-done | bytes 4194320 | tf_op jit(solution)/shard_map/all_gather | solution.py:146
  65.1 43.3 %while.99 = (s32[]{:T(128)}, f32[256,256]{1,0:T(8,128)S(1)}, f32[256]{0:T(256)S(1)}, f32[16,256,256]{2,1,0:T(8,128)}, f32[16,256]{1,0:T(8,128)S(1)}, /*index=5*/s32[]{:T(128)}, s32[]{:T(128)}) while((s32[]{:T(128)}, f32[256,256]{1,0:T(8,128)S(1)}, f32[256]{0:T(256)S(1)}, f32[16,256,256]{2,1,0:T(8,128)}, f32[16,256]{1,0:T(8,128)S(1)}, ...), condition=%wide.region_1.2_spmd.clone, body=%wide.region_0.1_spmd.clone.sunk | while | flops 202113536 | bytes 1583195 | solution.py:77
  108.5 329.0 %while.98 = (s32[]{:T(128)}, f32[256,256]{1,0:T(8,128)S(1)}, f32[256]{0:T(256)S(1)}, pred[]{:T(512)}, f32[256,256]{1,0:T(8,128)S(1)}, /*index=5*/f32[256]{0:T(256)S(1)}, s32[]{:T(128)}) while((s32[]{:T(128)}, f32[256,256]{1,0:T(8,128)S(1)}, f32[256]{0:T(256)S(1)}, pred[]{:T(512)}, f32[256,256]{1,0:T(8,128)S(1)}, ...), condition=%wide.region_3.4_spmd.clone, body=%wide.region_2.3_spmd.clone.sunk | while | flops 202375936 | bytes 3159159 | solution.py:165
  127.8 6.5 collective-permute-start
  138.5 6.5 collective-permute-start
  149.2 6.5 collective-permute-start
  159.9 6.5 collective-permute-start
  170.6 6.5 collective-permute-start
  181.3 6.5 collective-permute-start
  192.1 6.5 collective-permute-start
  213.5 6.5 collective-permute-start
  234.9 6.5 collective-permute-start
  245.6 6.5 collective-permute-start
  256.3 6.5 collective-permute-start
  267.0 6.5 collective-permute-start
  277.7 6.5 collective-permute-start
  288.4 6.5 collective-permute-start
  299.1 6.5 collective-permute-start
  320.5 6.5 collective-permute-start
  331.2 6.5 collective-permute-start
  341.9 6.5 collective-permute-start
  352.6 6.5 collective-permute-start
  363.3 6.5 collective-permute-start
  374.0 6.5 collective-permute-start
  384.7 6.5 collective-permute-start
  395.4 6.5 collective-permute-start
  406.1 6.5 collective-permute-start
  427.5 6.5 collective-permute-start
  437.8 21.9 %while.96 = (s32[]{:T(128)}, f32[256]{0:T(256)S(1)}, f32[16,256]{1,0:T(8,128)S(1)}, f32[16,256,256]{2,1,0:T(8,128)}, f32[16,256]{1,0:T(8,128)S(1)}, /*index=5*/s32[]{:T(128)}, s32[]{:T(128)}) while((s32[]{:T(128)}, f32[256]{0:T(256)S(1)}, f32[16,256]{1,0:T(8,128)S(1)}, f32[16,256,256]{2,1,0:T(8,128)}, f32[16,256]{1,0:T(8,128)S(1)}, ...), condition=%wide.region_5.6_spmd, body=%wide.region_4.5_spmd.sunk | while | flops 786690 | bytes 271957 | solution.py:87
  487.6 88.0 %while.100 = (s32[]{:T(128)}, f32[256,256]{1,0:T(8,128)S(1)}, f32[256,256]{1,0:T(8,128)S(1)}, f32[256]{0:T(256)S(1)}, f32[16,256,256]{2,1,0:T(8,128)}, /*index=5...) while((s32[]{:T(128)}, f32[256,256]{1,0:T(8,128)S(1)}, ...), condition=%wide.region_7.8_spmd.clone, body=%wide.region_6.7_spmd.clone.sunk | while | flops 604897792 | bytes 3418252 | solution.py:97
  575.7 446.2 %while.101 = (s32[]{:T(128)}, f32[256,256]{1,0:T(8,128)S(1)}, f32[256,256]{1,0:T(8,128)S(1)}, f32[256]{0:T(256)S(1)}, pred[]{:T(512)}, /*index=5*/f32[256,256]{1...) while((s32[]{:T(128)}, f32[256,256]{1,0:T(8,128)S(1)}, ...), condition=%wide.region_9.10_spmd.clone, body=%wide.region_8.9_spmd.clone.sunk | while | flops 605422592 | bytes 7091353 | solution.py:179
  579.4 11.5 %collective-permute-done.1 = f32[513,256]{1,0:T(8,128)S(1)} collective-permute-done((f32[513,256]{1,0:T(8,128)S(1)}, f32[513,256]{1,0:T(8,128)S(1)}, u32[]{:S(2)}, u32[]{:S(2)}) %collective-permute-start.1) | collective-permute-done | bytes 525344 | tf_op jit(solution)/shard_map/while/body/eval_jaxpr/ppermute | solution.py:12
  594.5 10.8 collective-permute-done.1
  608.9 10.8 collective-permute-done.1
  623.2 10.8 collective-permute-done.1
  637.6 10.8 collective-permute-done.1
  652.0 10.8 collective-permute-done.1
  666.3 10.8 collective-permute-done.1
  680.7 10.8 collective-permute-done.1
  695.0 10.8 collective-permute-done.1
  709.4 10.8 collective-permute-done.1
  723.8 10.8 collective-permute-done.1
  738.1 10.8 collective-permute-done.1
  752.5 10.8 collective-permute-done.1
  766.8 10.8 collective-permute-done.1
  781.2 10.8 collective-permute-done.1
  795.6 10.8 collective-permute-done.1
  809.9 10.8 collective-permute-done.1
  824.3 10.8 collective-permute-done.1
  838.7 10.8 collective-permute-done.1
  853.0 10.8 collective-permute-done.1
  867.4 10.8 collective-permute-done.1
  881.7 10.8 collective-permute-done.1
  896.1 10.8 collective-permute-done.1
  910.5 10.8 collective-permute-done.1
  924.8 10.8 collective-permute-done.1
  939.2 10.8 collective-permute-done.1
  953.5 10.8 collective-permute-done.1
  967.9 10.8 collective-permute-done.1
  982.3 10.8 collective-permute-done.1
  996.6 10.8 collective-permute-done.1
  1011.0 10.8 collective-permute-done.1
  1024.3 77.5 %while.97 = (s32[]{:T(128)}, f32[256,256]{1,0:T(8,128)S(1)}, f32[256]{0:T(256)S(1)}, f32[16,256]{1,0:T(8,128)S(1)}, f32[16,256,256]{2,1,0:T(8,128)}, /*index=5*/...) while((s32[]{:T(128)}, f32[256,256]{1,0:T(8,128)S(1)}, ...), condition=%wide.region_11.12_spmd, body=%wide.region_10.11_spmd.sunk | while | flops 403505408 | bytes 2369673 | solution.py:112
  (961 shorter events, 545.2 us)
Async XLA Ops:
  7.2 58.0 %all-gather.9.cloned.1.call-start = ((), (), s32[]{:S(2)}) async-start(), calls=%async_computation.2 | async-start | bytes 5242880 | tf_op jit(solution)/shard_map/all_gather | solution.py:146
  14.2 445.7 %all-gather.5.cloned.1.call-start = ((), (), s32[]{:S(2)}) async-start(), calls=%async_computation | async-start | bytes 5242880 | tf_op jit(solution)/shard_map/all_gather | solution.py:148
  15.0 453.4 %all-gather.7.cloned.1.call-start = ((), (), s32[]{:S(2)}) async-start(), calls=%async_computation.1 | async-start | bytes 5242880 | tf_op jit(solution)/shard_map/all_gather | solution.py:149
  117.1 9.9 collective-permute-start
  127.8 9.9 collective-permute-start
  138.5 9.9 collective-permute-start
  149.2 9.9 collective-permute-start
  159.9 9.9 collective-permute-start
  170.6 9.9 collective-permute-start
  181.3 9.9 collective-permute-start
  192.1 9.9 collective-permute-start
  202.8 9.9 collective-permute-start
  213.5 9.9 collective-permute-start
  224.2 9.9 collective-permute-start
  234.9 9.9 collective-permute-start
  245.6 9.9 collective-permute-start
  256.3 9.9 collective-permute-start
  267.0 9.9 collective-permute-start
  277.7 9.9 collective-permute-start
  288.4 9.9 collective-permute-start
  299.1 9.9 collective-permute-start
  309.8 9.9 collective-permute-start
  320.5 9.9 collective-permute-start
  331.2 9.9 collective-permute-start
  341.9 9.9 collective-permute-start
  352.6 9.9 collective-permute-start
  363.3 9.9 collective-permute-start
  374.0 9.9 collective-permute-start
  384.7 9.9 collective-permute-start
  395.4 9.9 collective-permute-start
  406.1 9.9 collective-permute-start
  416.8 9.9 collective-permute-start
  427.5 9.9 collective-permute-start
  577.5 13.4 %collective-permute-start.1 = (f32[513,256]{1,0:T(8,128)S(1)}, f32[513,256]{1,0:T(8,128)S(1)}, u32[]{:S(2)}, u32[]{:S(2)}) collective-permute-start(f32[513,256]{1,0:T(8,128)S(1)} %pad_maximum_fusion.5), channel_id=1, source_target_pairs={{4,0},{8,4},{12,8},{16,12},{20,16},{24,20},{28,24},{32,28},{36,32}... | collective-permute-start | bytes 1575944 | tf_op jit(solution)/shard_map/while/body/eval_jaxpr/ppermute | solution.py:12
  592.6 12.7 %collective-permute-start.1 = (f32[513,256]{1,0:T(8,128)S(1)}, f32[513,256]{1,0:T(8,128)S(1)}, u32[]{:S(2)}, u32[]{:S(2)}) collective-permute-start(f32[513,256]{1,0:T(8,128)S(1)} %pad_maximum_fusion.5), channel_id=1, source_target_pairs={{4,0},{8,4},{12,8},{16,12},{20,16},{24,20},{28,24},{32,28},{36,32}... | collective-permute-start | bytes 1575944 | tf_op jit(solution)/shard_map/while/body/eval_jaxpr/ppermute | solution.py:12
  606.9 12.7 %collective-permute-start.1 = (f32[513,256]{1,0:T(8,128)S(1)}, f32[513,256]{1,0:T(8,128)S(1)}, u32[]{:S(2)}, u32[]{:S(2)}) collective-permute-start(f32[513,256]{1,0:T(8,128)S(1)} %pad_maximum_fusion.5), channel_id=1, source_target_pairs={{4,0},{8,4},{12,8},{16,12},{20,16},{24,20},{28,24},{32,28},{36,32}... | collective-permute-start | bytes 1575944 | tf_op jit(solution)/shard_map/while/body/eval_jaxpr/ppermute | solution.py:12
  621.3 12.7 %collective-permute-start.1 = (f32[513,256]{1,0:T(8,128)S(1)}, f32[513,256]{1,0:T(8,128)S(1)}, u32[]{:S(2)}, u32[]{:S(2)}) collective-permute-start(f32[513,256]{1,0:T(8,128)S(1)} %pad_maximum_fusion.5), channel_id=1, source_target_pairs={{4,0},{8,4},{12,8},{16,12},{20,16},{24,20},{28,24},{32,28},{36,32}... | collective-permute-start | bytes 1575944 | tf_op jit(solution)/shard_map/while/body/eval_jaxpr/ppermute | solution.py:12
  635.7 12.7 %collective-permute-start.1 = (f32[513,256]{1,0:T(8,128)S(1)}, f32[513,256]{1,0:T(8,128)S(1)}, u32[]{:S(2)}, u32[]{:S(2)}) collective-permute-start(f32[513,256]{1,0:T(8,128)S(1)} %pad_maximum_fusion.5), channel_id=1, source_target_pairs={{4,0},{8,4},{12,8},{16,12},{20,16},{24,20},{28,24},{32,28},{36,32}... | collective-permute-start | bytes 1575944 | tf_op jit(solution)/shard_map/while/body/eval_jaxpr/ppermute | solution.py:12
  650.0 12.7 %collective-permute-start.1 = (f32[513,256]{1,0:T(8,128)S(1)}, f32[513,256]{1,0:T(8,128)S(1)}, u32[]{:S(2)}, u32[]{:S(2)}) collective-permute-start(f32[513,256]{1,0:T(8,128)S(1)} %pad_maximum_fusion.5), channel_id=1, source_target_pairs={{4,0},{8,4},{12,8},{16,12},{20,16},{24,20},{28,24},{32,28},{36,32}... | collective-permute-start | bytes 1575944 | tf_op jit(solution)/shard_map/while/body/eval_jaxpr/ppermute | solution.py:12
  664.4 12.7 %collective-permute-start.1 = (f32[513,256]{1,0:T(8,128)S(1)}, f32[513,256]{1,0:T(8,128)S(1)}, u32[]{:S(2)}, u32[]{:S(2)}) collective-permute-start(f32[513,256]{1,0:T(8,128)S(1)} %pad_maximum_fusion.5), channel_id=1, source_target_pairs={{4,0},{8,4},{12,8},{16,12},{20,16},{24,20},{28,24},{32,28},{36,32}... | collective-permute-start | bytes 1575944 | tf_op jit(solution)/shard_map/while/body/eval_jaxpr/ppermute | solution.py:12
  678.7 12.7 %collective-permute-start.1 = (f32[513,256]{1,0:T(8,128)S(1)}, f32[513,256]{1,0:T(8,128)S(1)}, u32[]{:S(2)}, u32[]{:S(2)}) collective-permute-start(f32[513,256]{1,0:T(8,128)S(1)} %pad_maximum_fusion.5), channel_id=1, source_target_pairs={{4,0},{8,4},{12,8},{16,12},{20,16},{24,20},{28,24},{32,28},{36,32}... | collective-permute-start | bytes 1575944 | tf_op jit(solution)/shard_map/while/body/eval_jaxpr/ppermute | solution.py:12
  693.1 12.7 %collective-permute-start.1 = (f32[513,256]{1,0:T(8,128)S(1)}, f32[513,256]{1,0:T(8,128)S(1)}, u32[]{:S(2)}, u32[]{:S(2)}) collective-permute-start(f32[513,256]{1,0:T(8,128)S(1)} %pad_maximum_fusion.5), channel_id=1, source_target_pairs={{4,0},{8,4},{12,8},{16,12},{20,16},{24,20},{28,24},{32,28},{36,32}... | collective-permute-start | bytes 1575944 | tf_op jit(solution)/shard_map/while/body/eval_jaxpr/ppermute | solution.py:12
  707.5 12.7 %collective-permute-start.1 = (f32[513,256]{1,0:T(8,128)S(1)}, f32[513,256]{1,0:T(8,128)S(1)}, u32[]{:S(2)}, u32[]{:S(2)}) collective-permute-start(f32[513,256]{1,0:T(8,128)S(1)} %pad_maximum_fusion.5), channel_id=1, source_target_pairs={{4,0},{8,4},{12,8},{16,12},{20,16},{24,20},{28,24},{32,28},{36,32}... | collective-permute-start | bytes 1575944 | tf_op jit(solution)/shard_map/while/body/eval_jaxpr/ppermute | solution.py:12
  721.8 12.7 %collective-permute-start.1 = (f32[513,256]{1,0:T(8,128)S(1)}, f32[513,256]{1,0:T(8,128)S(1)}, u32[]{:S(2)}, u32[]{:S(2)}) collective-permute-start(f32[513,256]{1,0:T(8,128)S(1)} %pad_maximum_fusion.5), channel_id=1, source_target_pairs={{4,0},{8,4},{12,8},{16,12},{20,16},{24,20},{28,24},{32,28},{36,32}... | collective-permute-start | bytes 1575944 | tf_op jit(solution)/shard_map/while/body/eval_jaxpr/ppermute | solution.py:12
  736.2 12.7 %collective-permute-start.1 = (f32[513,256]{1,0:T(8,128)S(1)}, f32[513,256]{1,0:T(8,128)S(1)}, u32[]{:S(2)}, u32[]{:S(2)}) collective-permute-start(f32[513,256]{1,0:T(8,128)S(1)} %pad_maximum_fusion.5), channel_id=1, source_target_pairs={{4,0},{8,4},{12,8},{16,12},{20,16},{24,20},{28,24},{32,28},{36,32}... | collective-permute-start | bytes 1575944 | tf_op jit(solution)/shard_map/while/body/eval_jaxpr/ppermute | solution.py:12
  750.6 12.7 %collective-permute-start.1 = (f32[513,256]{1,0:T(8,128)S(1)}, f32[513,256]{1,0:T(8,128)S(1)}, u32[]{:S(2)}, u32[]{:S(2)}) collective-permute-start(f32[513,256]{1,0:T(8,128)S(1)} %pad_maximum_fusion.5), channel_id=1, source_target_pairs={{4,0},{8,4},{12,8},{16,12},{20,16},{24,20},{28,24},{32,28},{36,32}... | collective-permute-start | bytes 1575944 | tf_op jit(solution)/shard_map/while/body/eval_jaxpr/ppermute | solution.py:12
  764.9 12.7 %collective-permute-start.1 = (f32[513,256]{1,0:T(8,128)S(1)}, f32[513,256]{1,0:T(8,128)S(1)}, u32[]{:S(2)}, u32[]{:S(2)}) collective-permute-start(f32[513,256]{1,0:T(8,128)S(1)} %pad_maximum_fusion.5), channel_id=1, source_target_pairs={{4,0},{8,4},{12,8},{16,12},{20,16},{24,20},{28,24},{32,28},{36,32}... | collective-permute-start | bytes 1575944 | tf_op jit(solution)/shard_map/while/body/eval_jaxpr/ppermute | solution.py:12
  779.3 12.7 %collective-permute-start.1 = (f32[513,256]{1,0:T(8,128)S(1)}, f32[513,256]{1,0:T(8,128)S(1)}, u32[]{:S(2)}, u32[]{:S(2)}) collective-permute-start(f32[513,256]{1,0:T(8,128)S(1)} %pad_maximum_fusion.5), channel_id=1, source_target_pairs={{4,0},{8,4},{12,8},{16,12},{20,16},{24,20},{28,24},{32,28},{36,32}... | collective-permute-start | bytes 1575944 | tf_op jit(solution)/shard_map/while/body/eval_jaxpr/ppermute | solution.py:12
  793.6 12.7 %collective-permute-start.1 = (f32[513,256]{1,0:T(8,128)S(1)}, f32[513,256]{1,0:T(8,128)S(1)}, u32[]{:S(2)}, u32[]{:S(2)}) collective-permute-start(f32[513,256]{1,0:T(8,128)S(1)} %pad_maximum_fusion.5), channel_id=1, source_target_pairs={{4,0},{8,4},{12,8},{16,12},{20,16},{24,20},{28,24},{32,28},{36,32}... | collective-permute-start | bytes 1575944 | tf_op jit(solution)/shard_map/while/body/eval_jaxpr/ppermute | solution.py:12
  808.0 12.7 %collective-permute-start.1 = (f32[513,256]{1,0:T(8,128)S(1)}, f32[513,256]{1,0:T(8,128)S(1)}, u32[]{:S(2)}, u32[]{:S(2)}) collective-permute-start(f32[513,256]{1,0:T(8,128)S(1)} %pad_maximum_fusion.5), channel_id=1, source_target_pairs={{4,0},{8,4},{12,8},{16,12},{20,16},{24,20},{28,24},{32,28},{36,32}... | collective-permute-start | bytes 1575944 | tf_op jit(solution)/shard_map/while/body/eval_jaxpr/ppermute | solution.py:12
  822.4 12.7 %collective-permute-start.1 = (f32[513,256]{1,0:T(8,128)S(1)}, f32[513,256]{1,0:T(8,128)S(1)}, u32[]{:S(2)}, u32[]{:S(2)}) collective-permute-start(f32[513,256]{1,0:T(8,128)S(1)} %pad_maximum_fusion.5), channel_id=1, source_target_pairs={{4,0},{8,4},{12,8},{16,12},{20,16},{24,20},{28,24},{32,28},{36,32}... | collective-permute-start | bytes 1575944 | tf_op jit(solution)/shard_map/while/body/eval_jaxpr/ppermute | solution.py:12
  836.7 12.7 %collective-permute-start.1 = (f32[513,256]{1,0:T(8,128)S(1)}, f32[513,256]{1,0:T(8,128)S(1)}, u32[]{:S(2)}, u32[]{:S(2)}) collective-permute-start(f32[513,256]{1,0:T(8,128)S(1)} %pad_maximum_fusion.5), channel_id=1, source_target_pairs={{4,0},{8,4},{12,8},{16,12},{20,16},{24,20},{28,24},{32,28},{36,32}... | collective-permute-start | bytes 1575944 | tf_op jit(solution)/shard_map/while/body/eval_jaxpr/ppermute | solution.py:12
  851.1 12.7 %collective-permute-start.1 = (f32[513,256]{1,0:T(8,128)S(1)}, f32[513,256]{1,0:T(8,128)S(1)}, u32[]{:S(2)}, u32[]{:S(2)}) collective-permute-start(f32[513,256]{1,0:T(8,128)S(1)} %pad_maximum_fusion.5), channel_id=1, source_target_pairs={{4,0},{8,4},{12,8},{16,12},{20,16},{24,20},{28,24},{32,28},{36,32}... | collective-permute-start | bytes 1575944 | tf_op jit(solution)/shard_map/while/body/eval_jaxpr/ppermute | solution.py:12
  865.4 12.7 %collective-permute-start.1 = (f32[513,256]{1,0:T(8,128)S(1)}, f32[513,256]{1,0:T(8,128)S(1)}, u32[]{:S(2)}, u32[]{:S(2)}) collective-permute-start(f32[513,256]{1,0:T(8,128)S(1)} %pad_maximum_fusion.5), channel_id=1, source_target_pairs={{4,0},{8,4},{12,8},{16,12},{20,16},{24,20},{28,24},{32,28},{36,32}... | collective-permute-start | bytes 1575944 | tf_op jit(solution)/shard_map/while/body/eval_jaxpr/ppermute | solution.py:12
  879.8 12.7 %collective-permute-start.1 = (f32[513,256]{1,0:T(8,128)S(1)}, f32[513,256]{1,0:T(8,128)S(1)}, u32[]{:S(2)}, u32[]{:S(2)}) collective-permute-start(f32[513,256]{1,0:T(8,128)S(1)} %pad_maximum_fusion.5), channel_id=1, source_target_pairs={{4,0},{8,4},{12,8},{16,12},{20,16},{24,20},{28,24},{32,28},{36,32}... | collective-permute-start | bytes 1575944 | tf_op jit(solution)/shard_map/while/body/eval_jaxpr/ppermute | solution.py:12
  894.2 12.7 %collective-permute-start.1 = (f32[513,256]{1,0:T(8,128)S(1)}, f32[513,256]{1,0:T(8,128)S(1)}, u32[]{:S(2)}, u32[]{:S(2)}) collective-permute-start(f32[513,256]{1,0:T(8,128)S(1)} %pad_maximum_fusion.5), channel_id=1, source_target_pairs={{4,0},{8,4},{12,8},{16,12},{20,16},{24,20},{28,24},{32,28},{36,32}... | collective-permute-start | bytes 1575944 | tf_op jit(solution)/shard_map/while/body/eval_jaxpr/ppermute | solution.py:12
  908.5 12.7 %collective-permute-start.1 = (f32[513,256]{1,0:T(8,128)S(1)}, f32[513,256]{1,0:T(8,128)S(1)}, u32[]{:S(2)}, u32[]{:S(2)}) collective-permute-start(f32[513,256]{1,0:T(8,128)S(1)} %pad_maximum_fusion.5), channel_id=1, source_target_pairs={{4,0},{8,4},{12,8},{16,12},{20,16},{24,20},{28,24},{32,28},{36,32}... | collective-permute-start | bytes 1575944 | tf_op jit(solution)/shard_map/while/body/eval_jaxpr/ppermute | solution.py:12
  922.9 12.7 %collective-permute-start.1 = (f32[513,256]{1,0:T(8,128)S(1)}, f32[513,256]{1,0:T(8,128)S(1)}, u32[]{:S(2)}, u32[]{:S(2)}) collective-permute-start(f32[513,256]{1,0:T(8,128)S(1)} %pad_maximum_fusion.5), channel_id=1, source_target_pairs={{4,0},{8,4},{12,8},{16,12},{20,16},{24,20},{28,24},{32,28},{36,32}... | collective-permute-start | bytes 1575944 | tf_op jit(solution)/shard_map/while/body/eval_jaxpr/ppermute | solution.py:12
  937.3 12.7 %collective-permute-start.1 = (f32[513,256]{1,0:T(8,128)S(1)}, f32[513,256]{1,0:T(8,128)S(1)}, u32[]{:S(2)}, u32[]{:S(2)}) collective-permute-start(f32[513,256]{1,0:T(8,128)S(1)} %pad_maximum_fusion.5), channel_id=1, source_target_pairs={{4,0},{8,4},{12,8},{16,12},{20,16},{24,20},{28,24},{32,28},{36,32}... | collective-permute-start | bytes 1575944 | tf_op jit(solution)/shard_map/while/body/eval_jaxpr/ppermute | solution.py:12
  951.6 12.7 %collective-permute-start.1 = (f32[513,256]{1,0:T(8,128)S(1)}, f32[513,256]{1,0:T(8,128)S(1)}, u32[]{:S(2)}, u32[]{:S(2)}) collective-permute-start(f32[513,256]{1,0:T(8,128)S(1)} %pad_maximum_fusion.5), channel_id=1, source_target_pairs={{4,0},{8,4},{12,8},{16,12},{20,16},{24,20},{28,24},{32,28},{36,32}... | collective-permute-start | bytes 1575944 | tf_op jit(solution)/shard_map/while/body/eval_jaxpr/ppermute | solution.py:12
  966.0 12.7 %collective-permute-start.1 = (f32[513,256]{1,0:T(8,128)S(1)}, f32[513,256]{1,0:T(8,128)S(1)}, u32[]{:S(2)}, u32[]{:S(2)}) collective-permute-start(f32[513,256]{1,0:T(8,128)S(1)} %pad_maximum_fusion.5), channel_id=1, source_target_pairs={{4,0},{8,4},{12,8},{16,12},{20,16},{24,20},{28,24},{32,28},{36,32}... | collective-permute-start | bytes 1575944 | tf_op jit(solution)/shard_map/while/body/eval_jaxpr/ppermute | solution.py:12
  980.3 12.7 %collective-permute-start.1 = (f32[513,256]{1,0:T(8,128)S(1)}, f32[513,256]{1,0:T(8,128)S(1)}, u32[]{:S(2)}, u32[]{:S(2)}) collective-permute-start(f32[513,256]{1,0:T(8,128)S(1)} %pad_maximum_fusion.5), channel_id=1, source_target_pairs={{4,0},{8,4},{12,8},{16,12},{20,16},{24,20},{28,24},{32,28},{36,32}... | collective-permute-start | bytes 1575944 | tf_op jit(solution)/shard_map/while/body/eval_jaxpr/ppermute | solution.py:12
  994.7 12.7 %collective-permute-start.1 = (f32[513,256]{1,0:T(8,128)S(1)}, f32[513,256]{1,0:T(8,128)S(1)}, u32[]{:S(2)}, u32[]{:S(2)}) collective-permute-start(f32[513,256]{1,0:T(8,128)S(1)} %pad_maximum_fusion.5), channel_id=1, source_target_pairs={{4,0},{8,4},{12,8},{16,12},{20,16},{24,20},{28,24},{32,28},{36,32}... | collective-permute-start | bytes 1575944 | tf_op jit(solution)/shard_map/while/body/eval_jaxpr/ppermute | solution.py:12
  1009.1 12.7 %collective-permute-start.1 = (f32[513,256]{1,0:T(8,128)S(1)}, f32[513,256]{1,0:T(8,128)S(1)}, u32[]{:S(2)}, u32[]{:S(2)}) collective-permute-start(f32[513,256]{1,0:T(8,128)S(1)} %pad_maximum_fusion.5), channel_id=1, source_target_pairs={{4,0},{8,4},{12,8},{16,12},{20,16},{24,20},{28,24},{32,28},{36,32}... | collective-permute-start | bytes 1575944 | tf_op jit(solution)/shard_map/while/body/eval_jaxpr/ppermute | solution.py:12
  (12 other events, 517.1 us)
Sparse Core Ops, SparseCore 0:
  14.3 50.7 all-gather.8
  66.8 48.9 all-gather.4
  117.5 48.4 all-gather.6
where the time goes:
time: 1120 us; the launch traced here: 1110 us
  waiting for transfers between devices  478 us (43%)
  matrix products  317 us (28%)
  starting transfers between devices  258 us (23%)
  local copies, waits for them, and re-layouts  16.4 us (1%)
  between operations  14.1 us (1%)
    ppermute x62, waiting for transfers between devices, from_behind(): return lax.ppermute(block, axis, route)  439 us
    dot_general x353, matrix products, matmul(): return jnp.matmul(left, right, precision=highest)  312 us
    ppermute x62, starting transfers between devices, from_behind(): return lax.ppermute(block, axis, route)  258 us
    all_gather x1, waiting for transfers between devices, per_device(): lax.all_gather(map_rows, 'blk', axis=1, tiled=True)  36.9 us
  transfers between devices with their start and end apart: 65, of which 63 were waited for; matrix products, arithmetic and copies ran while one was open for 9% of the time, Pallas kernels for 0%

commit v1 on v0

--- a/solution.py
+++ b/solution.py
@@ -143,7 +143,9 @@
     zero_mat = jnp.zeros((width, width), jnp.float32)
     zero_vec = jnp.zeros((width,), jnp.float32)
     transition_operators, step_shifts, gain_full, cov_full = (
-        lax.all_gather(map_rows, "blk", axis=1, tiled=True),
+        jnp.concatenate(
+            lax.all_to_all(jnp.stack([map_rows] * lax.axis_size("blk")), "blk", 0, 0), axis=1
+        ),
         lax.all_gather(shift_rows, "blk", axis=1, tiled=True),
         lax.all_gather(smooth_gains, "blk", axis=1, tiled=True),
         lax.all_gather(filt_cov, "blk", axis=1, tiled=True),

time: 1120 us -> 1170 us (1.045)
  blocking collectives: 10.5 us -> 84.3 us
  waiting for transfers between devices: 478 us -> 441 us
    all_gather x1, blocking collectives: 10.5 us -> 84.3 us  [per_device(): lax.all_gather(shift_rows, 'blk', axis=1, tiled=True)]
    all_gather x1 -> x0, waiting for transfers between devices: 36.9 us -> none  [per_device(): lax.all_gather(map_rows, 'blk', axis=1, tiled=True)]
  transfers between devices with their start and end apart: 65 -> 65, of which waited for: 63 -> 62; matrix products, arithmetic and copies ran while one was open for 9% -> 9% of each run, Pallas kernels for 0% -> 0%
where the time goes in v1:
time: 1170 us; the launch traced here: 1160 us
  waiting for transfers between devices  441 us (38%)
  matrix products  316 us (27%)
  starting transfers between devices  266 us (23%)
  blocking collectives  84.3 us (7%)
  local copies, waits for them, and re-layouts  23.3 us (2%)
  between operations  14.4 us (1%)
    ppermute x62, waiting for transfers between devices, from_behind(): return lax.ppermute(block, axis, route)  439 us
    dot_general x353, matrix products, matmul(): return jnp.matmul(left, right, precision=highest)  311 us
    ppermute x62, starting transfers between devices, from_behind(): return lax.ppermute(block, axis, route)  261 us
    all_gather x1, blocking collectives, per_device(): lax.all_gather(shift_rows, 'blk', axis=1, tiled=True)  84.3 us
  transfers between devices with their start and end apart: 65, of which 62 were waited for; matrix products, arithmetic and copies ran while one was open for 9% of the time, Pallas kernels for 0%

profile of v1, /device:TPU:7, one launch (start us, length us, event | category | flops | bytes accessed | tf_op | source)
XLA Modules:
  0.0 1161.6 jit_solution(7024248650072272359)
XLA Ops:
  23.3 84.3 %all-gather = f32[4,64,16]{1,2,0:T(8,128)S(1)} all-gather(f32[1,64,16]{1,2,0:T(8,128)S(1)} %bitcast.262), channel_id=1, replica_groups=mesh['tm'=32,'blk'=4] {'blk'}, dimensions={0}, use_global_device_ids=true | all-gather | bytes 20480 | tf_op jit(solution)/shard_map/all_gather | solution.py:149
  112.5 43.4 %while.99 = (s32[]{:T(128)}, f32[256,256]{1,0:T(8,128)S(1)}, f32[256]{0:T(256)S(1)}, f32[16,256,256]{2,1,0:T(8,128)}, f32[16,256]{1,0:T(8,128)S(1)}, /*index=5*/s32[]{:T(128)}, s32[]{:T(128)}) while((s32[]{:T(128)}, f32[256,256]{1,0:T(8,128)S(1)}, f32[256]{0:T(256)S(1)}, f32[16,256,256]{2,1,0:T(8,128)}, f32[16,256]{1,0:T(8,128)S(1)}, ...), condition=%wide.region_1.2_spmd.clone, body=%wide.region_0.1_spmd.clone.sunk | while | flops 202113536 | bytes 1583195 | solution.py:77
  156.0 331.5 %while.98 = (s32[]{:T(128)}, f32[256,256]{1,0:T(8,128)S(1)}, f32[256]{0:T(256)S(1)}, pred[]{:T(512)}, f32[256,256]{1,0:T(8,128)S(1)}, /*index=5*/f32[256]{0:T(256)S(1)}, s32[]{:T(128)}) while((s32[]{:T(128)}, f32[256,256]{1,0:T(8,128)S(1)}, f32[256]{0:T(256)S(1)}, pred[]{:T(512)}, f32[256,256]{1,0:T(8,128)S(1)}, ...), condition=%wide.region_3.4_spmd.clone, body=%wide.region_2.3_spmd.clone.sunk | while | flops 202375936 | bytes 3159159 | solution.py:167
  167.1 6.5 collective-permute-start
  177.8 6.5 collective-permute-start
  188.5 6.5 collective-permute-start
  199.2 6.5 collective-permute-start
  220.6 6.5 collective-permute-start
  231.4 6.5 collective-permute-start
  242.1 6.5 collective-permute-start
  252.8 6.5 collective-permute-start
  263.5 6.5 collective-permute-start
  274.2 6.5 collective-permute-start
  284.9 6.5 collective-permute-start
  295.6 6.5 collective-permute-start
  306.3 6.5 collective-permute-start
  327.7 6.5 collective-permute-start
  338.4 6.5 collective-permute-start
  349.1 6.5 collective-permute-start
  359.8 6.5 collective-permute-start
  370.5 6.5 collective-permute-start
  381.2 6.5 collective-permute-start
  391.9 6.5 collective-permute-start
  402.6 6.5 collective-permute-start
  413.3 6.5 collective-permute-start
  434.7 6.5 collective-permute-start
  445.4 6.5 collective-permute-start
  456.1 6.5 collective-permute-start
  477.5 6.5 collective-permute-start
  487.8 21.9 %while.96 = (s32[]{:T(128)}, f32[256]{0:T(256)S(1)}, f32[16,256]{1,0:T(8,128)S(1)}, f32[16,256,256]{2,1,0:T(8,128)}, f32[16,256]{1,0:T(8,128)S(1)}, /*index=5*/s32[]{:T(128)}, s32[]{:T(128)}) while((s32[]{:T(128)}, f32[256]{0:T(256)S(1)}, f32[16,256]{1,0:T(8,128)S(1)}, f32[16,256,256]{2,1,0:T(8,128)}, f32[16,256]{1,0:T(8,128)S(1)}, ...), condition=%wide.region_5.6_spmd, body=%wide.region_4.5_spmd.sunk | while | flops 786690 | bytes 271957 | solution.py:87
  537.6 88.0 %while.100 = (s32[]{:T(128)}, f32[256,256]{1,0:T(8,128)S(1)}, f32[256,256]{1,0:T(8,128)S(1)}, f32[256]{0:T(256)S(1)}, f32[16,256,256]{2,1,0:T(8,128)}, /*index=5...) while((s32[]{:T(128)}, f32[256,256]{1,0:T(8,128)S(1)}, ...), condition=%wide.region_7.8_spmd.clone, body=%wide.region_6.7_spmd.clone.sunk | while | flops 604897792 | bytes 3418252 | solution.py:97
  625.7 446.2 %while.101 = (s32[]{:T(128)}, f32[256,256]{1,0:T(8,128)S(1)}, f32[256,256]{1,0:T(8,128)S(1)}, f32[256]{0:T(256)S(1)}, pred[]{:T(512)}, /*index=5*/f32[256,256]{1...) while((s32[]{:T(128)}, f32[256,256]{1,0:T(8,128)S(1)}, ...), condition=%wide.region_9.10_spmd.clone, body=%wide.region_8.9_spmd.clone.sunk | while | flops 605422592 | bytes 7091353 | solution.py:181
  629.4 11.5 collective-permute-done.1
  644.5 10.8 collective-permute-done.1
  658.9 10.8 collective-permute-done.1
  673.3 10.8 collective-permute-done.1
  687.6 10.8 collective-permute-done.1
  702.0 10.8 collective-permute-done.1
  716.3 10.8 collective-permute-done.1
  730.7 10.8 collective-permute-done.1
  745.1 10.8 collective-permute-done.1
  759.4 10.8 collective-permute-done.1
  773.8 10.8 collective-permute-done.1
  788.1 10.8 collective-permute-done.1
  802.5 10.8 collective-permute-done.1
  816.9 10.8 collective-permute-done.1
  831.2 10.8 collective-permute-done.1
  845.6 10.8 collective-permute-done.1
  860.0 10.8 collective-permute-done.1
  874.3 10.8 collective-permute-done.1
  888.7 10.8 collective-permute-done.1
  903.0 10.8 collective-permute-done.1
  917.4 10.8 collective-permute-done.1
  931.8 10.8 collective-permute-done.1
  946.1 10.8 collective-permute-done.1
  960.5 10.8 collective-permute-done.1
  974.8 10.8 collective-permute-done.1
  989.2 10.8 collective-permute-done.1
  1003.6 10.8 collective-permute-done.1
  1017.9 10.8 collective-permute-done.1
  1032.3 10.8 collective-permute-done.1
  1046.6 10.8 collective-permute-done.1
  1061.0 10.8 collective-permute-done.1
  1074.3 77.6 %while.97 = (s32[]{:T(128)}, f32[256,256]{1,0:T(8,128)S(1)}, f32[256]{0:T(256)S(1)}, f32[16,256]{1,0:T(8,128)S(1)}, f32[16,256,256]{2,1,0:T(8,128)}, /*index=5*/...) while((s32[]{:T(128)}, f32[256,256]{1,0:T(8,128)S(1)}, ...), condition=%wide.region_11.12_spmd, body=%wide.region_10.11_spmd.sunk | while | flops 403505408 | bytes 2369673 | solution.py:112
  (961 shorter events, 551.8 us)
Async XLA Ops:
  7.2 502.7 %all-gather.4.cloned.1.call-start = ((), (), s32[]{:S(2)}) async-start(), calls=%async_computation.1 | async-start | bytes 5242880 | tf_op jit(solution)/shard_map/all_gather | solution.py:150
  16.3 91.5 %all-to-all-start = ((f32[4,16,64,256]{3,2,1,0:T(8,128)}), f32[4,16,64,256]{3,2,1,0:T(8,128)}, u32[]{:S(2)}, u32[]{:S(2)}) async-start(f32[4,16,64,256]{3,2,1,0:T(8,128)} %stack.2), calls=%async_computation | async-start | bytes 8388608 | tf_op jit(solution)/shard_map/all_to_all | solution.py:147
  21.5 496.8 %all-gather.6.cloned.1.call-start = ((), (), s32[]{:S(2)}) async-start(), calls=%async_computation.2 | async-start | bytes 5242880 | tf_op jit(solution)/shard_map/all_gather | solution.py:151
  167.1 9.9 collective-permute-start
  177.8 9.9 collective-permute-start
  188.5 9.9 collective-permute-start
  199.2 9.9 collective-permute-start
  209.9 9.9 collective-permute-start
  220.6 9.9 collective-permute-start
  231.4 9.9 collective-permute-start
  242.1 9.9 collective-permute-start
  252.8 9.9 collective-permute-start
  263.5 9.9 collective-permute-start
  274.2 9.9 collective-permute-start
  284.9 9.9 collective-permute-start
  295.6 9.9 collective-permute-start
  306.3 9.9 collective-permute-start
  317.0 9.9 collective-permute-start
  327.7 9.9 collective-permute-start
  338.4 9.9 collective-permute-start
  349.1 9.9 collective-permute-start
  359.8 9.9 collective-permute-start
  370.5 9.9 collective-permute-start
  381.2 9.9 collective-permute-start
  391.9 9.9 collective-permute-start
  402.6 9.9 collective-permute-start
  413.3 9.9 collective-permute-start
  424.0 9.9 collective-permute-start
  434.7 9.9 collective-permute-start
  445.4 9.9 collective-permute-start
  456.1 9.9 collective-permute-start
  466.8 9.9 collective-permute-start
  477.5 9.9 collective-permute-start
  627.5 13.5 %collective-permute-start.1 = (f32[513,256]{1,0:T(8,128)S(1)}, f32[513,256]{1,0:T(8,128)S(1)}, u32[]{:S(2)}, u32[]{:S(2)}) collective-permute-start(f32[513,256]{1,0:T(8,128)S(1)} %pad_maximum_fusion.5), channel_id=1, source_target_pairs={{4,0},{8,4},{12,8},{16,12},{20,16},{24,20},{28,24},{32,28},{36,32}... | collective-permute-start | bytes 1575944 | tf_op jit(solution)/shard_map/while/body/eval_jaxpr/ppermute | solution.py:12
  642.6 12.7 %collective-permute-start.1 = (f32[513,256]{1,0:T(8,128)S(1)}, f32[513,256]{1,0:T(8,128)S(1)}, u32[]{:S(2)}, u32[]{:S(2)}) collective-permute-start(f32[513,256]{1,0:T(8,128)S(1)} %pad_maximum_fusion.5), channel_id=1, source_target_pairs={{4,0},{8,4},{12,8},{16,12},{20,16},{24,20},{28,24},{32,28},{36,32}... | collective-permute-start | bytes 1575944 | tf_op jit(solution)/shard_map/while/body/eval_jaxpr/ppermute | solution.py:12
  657.0 12.7 %collective-permute-start.1 = (f32[513,256]{1,0:T(8,128)S(1)}, f32[513,256]{1,0:T(8,128)S(1)}, u32[]{:S(2)}, u32[]{:S(2)}) collective-permute-start(f32[513,256]{1,0:T(8,128)S(1)} %pad_maximum_fusion.5), channel_id=1, source_target_pairs={{4,0},{8,4},{12,8},{16,12},{20,16},{24,20},{28,24},{32,28},{36,32}... | collective-permute-start | bytes 1575944 | tf_op jit(solution)/shard_map/while/body/eval_jaxpr/ppermute | solution.py:12
  671.3 12.7 %collective-permute-start.1 = (f32[513,256]{1,0:T(8,128)S(1)}, f32[513,256]{1,0:T(8,128)S(1)}, u32[]{:S(2)}, u32[]{:S(2)}) collective-permute-start(f32[513,256]{1,0:T(8,128)S(1)} %pad_maximum_fusion.5), channel_id=1, source_target_pairs={{4,0},{8,4},{12,8},{16,12},{20,16},{24,20},{28,24},{32,28},{36,32}... | collective-permute-start | bytes 1575944 | tf_op jit(solution)/shard_map/while/body/eval_jaxpr/ppermute | solution.py:12
  685.7 12.7 %collective-permute-start.1 = (f32[513,256]{1,0:T(8,128)S(1)}, f32[513,256]{1,0:T(8,128)S(1)}, u32[]{:S(2)}, u32[]{:S(2)}) collective-permute-start(f32[513,256]{1,0:T(8,128)S(1)} %pad_maximum_fusion.5), channel_id=1, source_target_pairs={{4,0},{8,4},{12,8},{16,12},{20,16},{24,20},{28,24},{32,28},{36,32}... | collective-permute-start | bytes 1575944 | tf_op jit(solution)/shard_map/while/body/eval_jaxpr/ppermute | solution.py:12
  700.1 12.7 %collective-permute-start.1 = (f32[513,256]{1,0:T(8,128)S(1)}, f32[513,256]{1,0:T(8,128)S(1)}, u32[]{:S(2)}, u32[]{:S(2)}) collective-permute-start(f32[513,256]{1,0:T(8,128)S(1)} %pad_maximum_fusion.5), channel_id=1, source_target_pairs={{4,0},{8,4},{12,8},{16,12},{20,16},{24,20},{28,24},{32,28},{36,32}... | collective-permute-start | bytes 1575944 | tf_op jit(solution)/shard_map/while/body/eval_jaxpr/ppermute | solution.py:12
  714.4 12.7 %collective-permute-start.1 = (f32[513,256]{1,0:T(8,128)S(1)}, f32[513,256]{1,0:T(8,128)S(1)}, u32[]{:S(2)}, u32[]{:S(2)}) collective-permute-start(f32[513,256]{1,0:T(8,128)S(1)} %pad_maximum_fusion.5), channel_id=1, source_target_pairs={{4,0},{8,4},{12,8},{16,12},{20,16},{24,20},{28,24},{32,28},{36,32}... | collective-permute-start | bytes 1575944 | tf_op jit(solution)/shard_map/while/body/eval_jaxpr/ppermute | solution.py:12
  728.8 12.7 %collective-permute-start.1 = (f32[513,256]{1,0:T(8,128)S(1)}, f32[513,256]{1,0:T(8,128)S(1)}, u32[]{:S(2)}, u32[]{:S(2)}) collective-permute-start(f32[513,256]{1,0:T(8,128)S(1)} %pad_maximum_fusion.5), channel_id=1, source_target_pairs={{4,0},{8,4},{12,8},{16,12},{20,16},{24,20},{28,24},{32,28},{36,32}... | collective-permute-start | bytes 1575944 | tf_op jit(solution)/shard_map/while/body/eval_jaxpr/ppermute | solution.py:12
  743.1 12.7 %collective-permute-start.1 = (f32[513,256]{1,0:T(8,128)S(1)}, f32[513,256]{1,0:T(8,128)S(1)}, u32[]{:S(2)}, u32[]{:S(2)}) collective-permute-start(f32[513,256]{1,0:T(8,128)S(1)} %pad_maximum_fusion.5), channel_id=1, source_target_pairs={{4,0},{8,4},{12,8},{16,12},{20,16},{24,20},{28,24},{32,28},{36,32}... | collective-permute-start | bytes 1575944 | tf_op jit(solution)/shard_map/while/body/eval_jaxpr/ppermute | solution.py:12
  757.5 12.7 %collective-permute-start.1 = (f32[513,256]{1,0:T(8,128)S(1)}, f32[513,256]{1,0:T(8,128)S(1)}, u32[]{:S(2)}, u32[]{:S(2)}) collective-permute-start(f32[513,256]{1,0:T(8,128)S(1)} %pad_maximum_fusion.5), channel_id=1, source_target_pairs={{4,0},{8,4},{12,8},{16,12},{20,16},{24,20},{28,24},{32,28},{36,32}... | collective-permute-start | bytes 1575944 | tf_op jit(solution)/shard_map/while/body/eval_jaxpr/ppermute | solution.py:12
  771.9 12.7 %collective-permute-start.1 = (f32[513,256]{1,0:T(8,128)S(1)}, f32[513,256]{1,0:T(8,128)S(1)}, u32[]{:S(2)}, u32[]{:S(2)}) collective-permute-start(f32[513,256]{1,0:T(8,128)S(1)} %pad_maximum_fusion.5), channel_id=1, source_target_pairs={{4,0},{8,4},{12,8},{16,12},{20,16},{24,20},{28,24},{32,28},{36,32}... | collective-permute-start | bytes 1575944 | tf_op jit(solution)/shard_map/while/body/eval_jaxpr/ppermute | solution.py:12
  786.2 12.7 %collective-permute-start.1 = (f32[513,256]{1,0:T(8,128)S(1)}, f32[513,256]{1,0:T(8,128)S(1)}, u32[]{:S(2)}, u32[]{:S(2)}) collective-permute-start(f32[513,256]{1,0:T(8,128)S(1)} %pad_maximum_fusion.5), channel_id=1, source_target_pairs={{4,0},{8,4},{12,8},{16,12},{20,16},{24,20},{28,24},{32,28},{36,32}... | collective-permute-start | bytes 1575944 | tf_op jit(solution)/shard_map/while/body/eval_jaxpr/ppermute | solution.py:12
  800.6 12.7 %collective-permute-start.1 = (f32[513,256]{1,0:T(8,128)S(1)}, f32[513,256]{1,0:T(8,128)S(1)}, u32[]{:S(2)}, u32[]{:S(2)}) collective-permute-start(f32[513,256]{1,0:T(8,128)S(1)} %pad_maximum_fusion.5), channel_id=1, source_target_pairs={{4,0},{8,4},{12,8},{16,12},{20,16},{24,20},{28,24},{32,28},{36,32}... | collective-permute-start | bytes 1575944 | tf_op jit(solution)/shard_map/while/body/eval_jaxpr/ppermute | solution.py:12
  814.9 12.7 %collective-permute-start.1 = (f32[513,256]{1,0:T(8,128)S(1)}, f32[513,256]{1,0:T(8,128)S(1)}, u32[]{:S(2)}, u32[]{:S(2)}) collective-permute-start(f32[513,256]{1,0:T(8,128)S(1)} %pad_maximum_fusion.5), channel_id=1, source_target_pairs={{4,0},{8,4},{12,8},{16,12},{20,16},{24,20},{28,24},{32,28},{36,32}... | collective-permute-start | bytes 1575944 | tf_op jit(solution)/shard_map/while/body/eval_jaxpr/ppermute | solution.py:12
  829.3 12.7 %collective-permute-start.1 = (f32[513,256]{1,0:T(8,128)S(1)}, f32[513,256]{1,0:T(8,128)S(1)}, u32[]{:S(2)}, u32[]{:S(2)}) collective-permute-start(f32[513,256]{1,0:T(8,128)S(1)} %pad_maximum_fusion.5), channel_id=1, source_target_pairs={{4,0},{8,4},{12,8},{16,12},{20,16},{24,20},{28,24},{32,28},{36,32}... | collective-permute-start | bytes 1575944 | tf_op jit(solution)/shard_map/while/body/eval_jaxpr/ppermute | solution.py:12
  843.7 12.7 %collective-permute-start.1 = (f32[513,256]{1,0:T(8,128)S(1)}, f32[513,256]{1,0:T(8,128)S(1)}, u32[]{:S(2)}, u32[]{:S(2)}) collective-permute-start(f32[513,256]{1,0:T(8,128)S(1)} %pad_maximum_fusion.5), channel_id=1, source_target_pairs={{4,0},{8,4},{12,8},{16,12},{20,16},{24,20},{28,24},{32,28},{36,32}... | collective-permute-start | bytes 1575944 | tf_op jit(solution)/shard_map/while/body/eval_jaxpr/ppermute | solution.py:12
  858.0 12.7 %collective-permute-start.1 = (f32[513,256]{1,0:T(8,128)S(1)}, f32[513,256]{1,0:T(8,128)S(1)}, u32[]{:S(2)}, u32[]{:S(2)}) collective-permute-start(f32[513,256]{1,0:T(8,128)S(1)} %pad_maximum_fusion.5), channel_id=1, source_target_pairs={{4,0},{8,4},{12,8},{16,12},{20,16},{24,20},{28,24},{32,28},{36,32}... | collective-permute-start | bytes 1575944 | tf_op jit(solution)/shard_map/while/body/eval_jaxpr/ppermute | solution.py:12
  872.4 12.7 %collective-permute-start.1 = (f32[513,256]{1,0:T(8,128)S(1)}, f32[513,256]{1,0:T(8,128)S(1)}, u32[]{:S(2)}, u32[]{:S(2)}) collective-permute-start(f32[513,256]{1,0:T(8,128)S(1)} %pad_maximum_fusion.5), channel_id=1, source_target_pairs={{4,0},{8,4},{12,8},{16,12},{20,16},{24,20},{28,24},{32,28},{36,32}... | collective-permute-start | bytes 1575944 | tf_op jit(solution)/shard_map/while/body/eval_jaxpr/ppermute | solution.py:12
  886.7 12.7 %collective-permute-start.1 = (f32[513,256]{1,0:T(8,128)S(1)}, f32[513,256]{1,0:T(8,128)S(1)}, u32[]{:S(2)}, u32[]{:S(2)}) collective-permute-start(f32[513,256]{1,0:T(8,128)S(1)} %pad_maximum_fusion.5), channel_id=1, source_target_pairs={{4,0},{8,4},{12,8},{16,12},{20,16},{24,20},{28,24},{32,28},{36,32}... | collective-permute-start | bytes 1575944 | tf_op jit(solution)/shard_map/while/body/eval_jaxpr/ppermute | solution.py:12
  901.1 12.7 %collective-permute-start.1 = (f32[513,256]{1,0:T(8,128)S(1)}, f32[513,256]{1,0:T(8,128)S(1)}, u32[]{:S(2)}, u32[]{:S(2)}) collective-permute-start(f32[513,256]{1,0:T(8,128)S(1)} %pad_maximum_fusion.5), channel_id=1, source_target_pairs={{4,0},{8,4},{12,8},{16,12},{20,16},{24,20},{28,24},{32,28},{36,32}... | collective-permute-start | bytes 1575944 | tf_op jit(solution)/shard_map/while/body/eval_jaxpr/ppermute | solution.py:12
  915.5 12.7 %collective-permute-start.1 = (f32[513,256]{1,0:T(8,128)S(1)}, f32[513,256]{1,0:T(8,128)S(1)}, u32[]{:S(2)}, u32[]{:S(2)}) collective-permute-start(f32[513,256]{1,0:T(8,128)S(1)} %pad_maximum_fusion.5), channel_id=1, source_target_pairs={{4,0},{8,4},{12,8},{16,12},{20,16},{24,20},{28,24},{32,28},{36,32}... | collective-permute-start | bytes 1575944 | tf_op jit(solution)/shard_map/while/body/eval_jaxpr/ppermute | solution.py:12
  929.8 12.7 %collective-permute-start.1 = (f32[513,256]{1,0:T(8,128)S(1)}, f32[513,256]{1,0:T(8,128)S(1)}, u32[]{:S(2)}, u32[]{:S(2)}) collective-permute-start(f32[513,256]{1,0:T(8,128)S(1)} %pad_maximum_fusion.5), channel_id=1, source_target_pairs={{4,0},{8,4},{12,8},{16,12},{20,16},{24,20},{28,24},{32,28},{36,32}... | collective-permute-start | bytes 1575944 | tf_op jit(solution)/shard_map/while/body/eval_jaxpr/ppermute | solution.py:12
  944.2 12.7 %collective-permute-start.1 = (f32[513,256]{1,0:T(8,128)S(1)}, f32[513,256]{1,0:T(8,128)S(1)}, u32[]{:S(2)}, u32[]{:S(2)}) collective-permute-start(f32[513,256]{1,0:T(8,128)S(1)} %pad_maximum_fusion.5), channel_id=1, source_target_pairs={{4,0},{8,4},{12,8},{16,12},{20,16},{24,20},{28,24},{32,28},{36,32}... | collective-permute-start | bytes 1575944 | tf_op jit(solution)/shard_map/while/body/eval_jaxpr/ppermute | solution.py:12
  958.6 12.7 %collective-permute-start.1 = (f32[513,256]{1,0:T(8,128)S(1)}, f32[513,256]{1,0:T(8,128)S(1)}, u32[]{:S(2)}, u32[]{:S(2)}) collective-permute-start(f32[513,256]{1,0:T(8,128)S(1)} %pad_maximum_fusion.5), channel_id=1, source_target_pairs={{4,0},{8,4},{12,8},{16,12},{20,16},{24,20},{28,24},{32,28},{36,32}... | collective-permute-start | bytes 1575944 | tf_op jit(solution)/shard_map/while/body/eval_jaxpr/ppermute | solution.py:12
  972.9 12.7 %collective-permute-start.1 = (f32[513,256]{1,0:T(8,128)S(1)}, f32[513,256]{1,0:T(8,128)S(1)}, u32[]{:S(2)}, u32[]{:S(2)}) collective-permute-start(f32[513,256]{1,0:T(8,128)S(1)} %pad_maximum_fusion.5), channel_id=1, source_target_pairs={{4,0},{8,4},{12,8},{16,12},{20,16},{24,20},{28,24},{32,28},{36,32}... | collective-permute-start | bytes 1575944 | tf_op jit(solution)/shard_map/while/body/eval_jaxpr/ppermute | solution.py:12
  987.3 12.7 %collective-permute-start.1 = (f32[513,256]{1,0:T(8,128)S(1)}, f32[513,256]{1,0:T(8,128)S(1)}, u32[]{:S(2)}, u32[]{:S(2)}) collective-permute-start(f32[513,256]{1,0:T(8,128)S(1)} %pad_maximum_fusion.5), channel_id=1, source_target_pairs={{4,0},{8,4},{12,8},{16,12},{20,16},{24,20},{28,24},{32,28},{36,32}... | collective-permute-start | bytes 1575944 | tf_op jit(solution)/shard_map/while/body/eval_jaxpr/ppermute | solution.py:12
  1001.6 12.7 %collective-permute-start.1 = (f32[513,256]{1,0:T(8,128)S(1)}, f32[513,256]{1,0:T(8,128)S(1)}, u32[]{:S(2)}, u32[]{:S(2)}) collective-permute-start(f32[513,256]{1,0:T(8,128)S(1)} %pad_maximum_fusion.5), channel_id=1, source_target_pairs={{4,0},{8,4},{12,8},{16,12},{20,16},{24,20},{28,24},{32,28},{36,32}... | collective-permute-start | bytes 1575944 | tf_op jit(solution)/shard_map/while/body/eval_jaxpr/ppermute | solution.py:12
  1016.0 12.7 %collective-permute-start.1 = (f32[513,256]{1,0:T(8,128)S(1)}, f32[513,256]{1,0:T(8,128)S(1)}, u32[]{:S(2)}, u32[]{:S(2)}) collective-permute-start(f32[513,256]{1,0:T(8,128)S(1)} %pad_maximum_fusion.5), channel_id=1, source_target_pairs={{4,0},{8,4},{12,8},{16,12},{20,16},{24,20},{28,24},{32,28},{36,32}... | collective-permute-start | bytes 1575944 | tf_op jit(solution)/shard_map/while/body/eval_jaxpr/ppermute | solution.py:12
  1030.4 12.7 %collective-permute-start.1 = (f32[513,256]{1,0:T(8,128)S(1)}, f32[513,256]{1,0:T(8,128)S(1)}, u32[]{:S(2)}, u32[]{:S(2)}) collective-permute-start(f32[513,256]{1,0:T(8,128)S(1)} %pad_maximum_fusion.5), channel_id=1, source_target_pairs={{4,0},{8,4},{12,8},{16,12},{20,16},{24,20},{28,24},{32,28},{36,32}... | collective-permute-start | bytes 1575944 | tf_op jit(solution)/shard_map/while/body/eval_jaxpr/ppermute | solution.py:12
  1044.7 12.7 %collective-permute-start.1 = (f32[513,256]{1,0:T(8,128)S(1)}, f32[513,256]{1,0:T(8,128)S(1)}, u32[]{:S(2)}, u32[]{:S(2)}) collective-permute-start(f32[513,256]{1,0:T(8,128)S(1)} %pad_maximum_fusion.5), channel_id=1, source_target_pairs={{4,0},{8,4},{12,8},{16,12},{20,16},{24,20},{28,24},{32,28},{36,32}... | collective-permute-start | bytes 1575944 | tf_op jit(solution)/shard_map/while/body/eval_jaxpr/ppermute | solution.py:12
  1059.1 12.7 %collective-permute-start.1 = (f32[513,256]{1,0:T(8,128)S(1)}, f32[513,256]{1,0:T(8,128)S(1)}, u32[]{:S(2)}, u32[]{:S(2)}) collective-permute-start(f32[513,256]{1,0:T(8,128)S(1)} %pad_maximum_fusion.5), channel_id=1, source_target_pairs={{4,0},{8,4},{12,8},{16,12},{20,16},{24,20},{28,24},{32,28},{36,32}... | collective-permute-start | bytes 1575944 | tf_op jit(solution)/shard_map/while/body/eval_jaxpr/ppermute | solution.py:12
  (12 other events, 681.5 us)
Sparse Core Ops, SparseCore 0:
  9.7 95.7 all-gather.3
  107.2 47.0 all-gather.5
